TPU v7x, 32 devices: a whole 2x2x4 slice. The times are simulated.
32 devices in a mesh: gy: 4 (over y, x), gx: 8 (over z, core).
Axes of the slice: x: 2, y: 2, z: 4, core: 2. Of those that a mesh axis runs over, the one named last changes fastest.
Arguments:
- window_starts: int32 [4, 8, 2, 4], P('gy', 'gx'), may hold values from -64 to 192, as said below
- slot_counts: int32 [4, 8], P('gy', 'gx'), may hold values from 2 to 4, as said below
- intensities: float32 [4, 8, 4, 128, 128], P('gy', 'gx'), may hold values from 0 to 1
- probe_field: float32 [2, 128, 128], replicated, may hold values from -3 to 3
- kernel_phase: float32 [128, 128], replicated, may hold values from -3.140625 to 3.140625
- object_field: float32 [2, 2, 1024, 2048], P(None, None, 'gy', 'gx'), may hold values from -4.2 to 4.2
Outputs:
- estimate: float32 [2, 2, 1024, 2048], P(None, None, 'gy', 'gx')
- gradient: float32 [2, 2, 1024, 2048], P(None, None, 'gy', 'gx')
Inputs may be any that keep to these rules, and one draw needn't show every extreme that they name: `slot_counts`: slots 0 to the count minus one of a tile are live, the rest unused. `window_starts`: A slot's window covers 128 x 128 cells from its start, in cells relative to the tile's first cell. In every tile, slot 0's window starts above the tile's first row and reaches past its last column; slot 1's window reaches past its last row and starts left of its first column.
All inputs are finite; a program needn't handle non-finite values.
Results may differ from a plain program's by a relative error of at most 0.0003.
Values sent between devices are 32-bit elements; how exact they have to be, the bound alone decides.
A program may use at most 64 MiB of HBM per device.

v0:
```python
import functools
import math

import jax
import jax.numpy as jnp
import numpy as np
from jax import lax
from jax.experimental import pallas as pl
from jax.experimental.pallas import tpu as pltpu
from jax.sharding import PartitionSpec as P

ITERS = 2
LANES = 128
MESH = pl.DeviceIdType.MESH

step_size = 0.5
HALO, FOLD = 0, 1
BACK, AHEAD = 0, 1


def split(table):
    high = table.astype(jnp.bfloat16)
    low = (table - high.astype(np.float32)).astype(jnp.bfloat16)
    return high, low


def fourier_tables(window):
    cells = np.arange(window)
    phase = 2.0 * math.pi / window * (cells[:, None] * cells[None, :] % window)
    real = np.cos(phase) / math.sqrt(window)
    rights, lefts = [], []
    for sign in (-1.0, 1.0):
        imag = sign * np.sin(phase) / math.sqrt(window)
        right = np.block([[real, imag], [-imag, real]]).astype(np.float32)
        high, low = split(right)
        rights.append(np.concatenate([high, high, low], axis=0))
        high, low = split(np.ascontiguousarray(right.T))
        lefts.append(np.concatenate([high, low, high], axis=1))
    return np.stack(rights), np.stack(lefts)


def halves(x):
    high = x.astype(jnp.bfloat16)
    low = (x - high.astype(jnp.float32)).astype(jnp.bfloat16)
    return high, low


def transform(fields, right, left):
    size = fields[0][0].shape[0]
    count = len(fields)
    rows = jnp.concatenate([jnp.concatenate(f, axis=1) for f in fields], axis=0)
    high, low = halves(rows)
    rows = jnp.dot(
        jnp.concatenate([high, low, high], axis=1), right[...], preferred_element_type=jnp.float32
    )
    cols = jnp.concatenate(
        [
            jnp.concatenate(
                [
                    rows[n * size : (n + 1) * size, :size],
                    rows[n * size : (n + 1) * size, size:],
                ],
                axis=0,
            )
            for n in range(count)
        ],
        axis=1,
    )
    high, low = halves(cols)
    cols = jnp.dot(
        left[...], jnp.concatenate([high, high, low], axis=0), preferred_element_type=jnp.float32
    )
    return [
        (cols[:size, n * size : (n + 1) * size], cols[size:, n * size : (n + 1) * size])
        for n in range(count)
    ]


def times(a, b):
    return (a[0] * b[0] - a[1] * b[1], a[0] * b[1] + a[1] * b[0])


def conj_times(a, b):
    return (a[0] * b[0] + a[1] * b[1], a[0] * b[1] - a[1] * b[0])


def kernel(
    sizes,
    starts_ref,
    count_ref,
    inten_ref,
    probe_ref,
    prop_ref,
    right_ref,
    left_ref,
    obj_ref,
    est_ref,
    grad_ref,
    ext,
    acc,
    row_pick,
    row_place,
    col_pick,
    col_place,
    col_out,
    col_in,
    row_in,
    send_sem,
    recv_sem,
):
    rows_axis, cols_axis, window = sizes
    tile = obj_ref.shape[-1]
    rim = window // 2
    slots = inten_ref.shape[2]
    rows_all = tile + 2 * rim
    lane0 = LANES
    inner = slice(lane0, lane0 + tile)
    wide = tile + 2 * LANES
    my, mx = lax.axis_index("gy"), lax.axis_index("gx")
    up = {"gy": lax.rem(my + rows_axis - 1, rows_axis)}
    down = {"gy": lax.rem(my + 1, rows_axis)}
    west = {"gx": lax.rem(mx + cols_axis - 1, cols_axis)}
    east = {"gx": lax.rem(mx + 1, cols_axis)}

    barrier = pltpu.get_barrier_semaphore()
    for other in (up, down, west, east):
        pl.semaphore_signal(barrier, inc=1, device_id=other, device_id_type=MESH)
    pl.semaphore_wait(barrier, 4)

    def remote(src, dst, it, what, s, part, direction):
        k = ((((it * 2) + what) * 2 + s) * 3 + part) * 2 + direction
        dev = ((west, east), (west, east), (up, down))[part][direction]
        return pltpu.make_async_remote_copy(
            src_ref=src,
            dst_ref=dst,
            send_sem=send_sem.at[k],
            recv_sem=recv_sem.at[k],
            device_id=dev,
            device_id_type=MESH,
        )

    def col_copy(it, what, s, part, direction):
        span = pl.ds(0, tile) if part == 0 else pl.ds(tile, 2 * rim)
        at = (it, what, s, direction, span)
        return remote(col_out.at[at], col_in.at[at], it, what, s, part, direction)

    def halo_rows(it, s, direction):
        first = 0 if direction == BACK else tile - rim
        if it == 0:
            src = obj_ref.at[s, :, pl.ds(first, rim), :]
        else:
            src = ext.at[it, s, :, pl.ds(rim + first, rim), pl.ds(lane0, tile)]
        land = tile + rim if direction == BACK else 0
        dst = ext.at[it, s, :, pl.ds(land, rim), pl.ds(lane0, tile)]
        return remote(src, dst, it, HALO, s, 2, direction)

    def fold_rows(it, s, direction):
        first = 0 if direction == BACK else tile + rim
        src = acc.at[it, s, :, pl.ds(first, rim), pl.ds(lane0, tile)]
        return remote(src, row_in.at[it, s, direction], it, FOLD, s, 2, direction)

    def low_lanes(shape):
        return lax.broadcasted_iota(jnp.int32, shape, 1) < rim

    def turned(x):
        return pltpu.roll(x, rim, 1)

    def pack_low(re, im):
        return jnp.where(low_lanes(re.shape), re, turned(im))

    def pack_high(re, im):
        return jnp.where(low_lanes(re.shape), turned(re), im)

    sent = []

    def start(copy):
        copy.start()
        sent.append(copy)

    mid_pieces = ((0, rim, tile),)
    rim_pieces = ((tile, 0, rim), (tile + rim, tile + rim, rim))

    def halo_cols(it, s, part):
        for at, first, length in mid_pieces if part == 0 else rim_pieces:
            src = ext.at[it, s]
            rows = pl.ds(first, length)
            re, im = (src[c, rows, lane0 : lane0 + LANES] for c in range(2))
            col_out[it, HALO, s, BACK, pl.ds(at, length), :] = pack_low(re, im)
            re, im = (src[c, rows, lane0 + tile - LANES : lane0 + tile] for c in range(2))
            col_out[it, HALO, s, AHEAD, pl.ds(at, length), :] = pack_high(re, im)
        for direction in (BACK, AHEAD):
            start(col_copy(it, HALO, s, part, direction))

    def unpack_halo(it, s):
        for at, first, length in mid_pieces + rim_pieces:
            rows = pl.ds(first, length)
            got = col_in[it, HALO, s, AHEAD, pl.ds(at, length), :]
            ext[it, s, 0, rows, 0:LANES] = turned(got)
            ext[it, s, 1, rows, 0:LANES] = got
            got = col_in[it, HALO, s, BACK, pl.ds(at, length), :]
            ext[it, s, 0, rows, lane0 + tile : wide] = got
            ext[it, s, 1, rows, lane0 + tile : wide] = turned(got)

    def halo_start(it, s):
        for direction in (BACK, AHEAD):
            start(halo_rows(it, s, direction))
        halo_cols(it, s, 0)

    def halo_corners(it, s):
        for direction in (BACK, AHEAD):
            halo_rows(it, s, direction).wait_recv()
        halo_cols(it, s, 1)

    def halo_finish(it, s):
        for part in (0, 1):
            for direction in (BACK, AHEAD):
                col_copy(it, HALO, s, part, direction).wait_recv()
        unpack_halo(it, s)

    def ones(mask):
        return jnp.where(mask, 1.0, 0.0).astype(jnp.bfloat16)

    def build_picks():
        for j in range(slots):
            row = starts_ref[0, 0, 0, j] + rim
            col = starts_ref[0, 0, 1, j] + lane0
            span = slice(j * window, (j + 1) * window)
            for ref, at, first, shape, sign in (
                (row_pick, (span, slice(None)), row, (window, rows_all), 1),
                (row_place, (slice(None), span), row, (rows_all, window), -1),
                (col_pick, (slice(None), span), col, (wide, window), -1),
                (col_place, (span, slice(None)), col, (window, wide), 1),
            ):
                across = lax.broadcasted_iota(jnp.int32, shape, 1)
                along = lax.broadcasted_iota(jnp.int32, shape, 0)
                live = jnp.full(shape, count_ref[0, 0], jnp.int32) > j
                ref[at] = ones((sign * (across - along) == first) & live)

    def crop(it, s):
        both = jnp.concatenate([ext[it, s, c] for c in range(2)], axis=0)
        high, low = halves(both)
        cols = jnp.dot(
            jnp.concatenate([high, low], axis=1),
            jnp.concatenate([col_pick[...], col_pick[...]], axis=0),
            preferred_element_type=jnp.float32,
        )
        high, low = halves(cols)
        out = []
        for j in range(slots):
            span = slice(j * window, (j + 1) * window)
            pick = row_pick[span, :]
            field = [
                jnp.concatenate([part[:rows_all, span], part[rows_all:, span]], axis=1)
                for part in (high, low)
            ]
            got = jnp.dot(
                jnp.concatenate([pick, pick], axis=1),
                jnp.concatenate(field, axis=0),
                preferred_element_type=jnp.float32,
            )
            out.append((got[:, :window], got[:, window:]))
        return out

    def scatter(it, s, grads):
        parts = []
        for j in range(slots):
            span = slice(j * window, (j + 1) * window)
            put = row_place[:, span]
            high, low = halves(jnp.concatenate(grads[j], axis=1))
            got = jnp.dot(
                jnp.concatenate([put, put], axis=1),
                jnp.concatenate([high, low], axis=0),
                preferred_element_type=jnp.float32,
            )
            parts.append(jnp.concatenate([got[:, :window], got[:, window:]], axis=0))
        high, low = halves(jnp.concatenate(parts, axis=1))
        total = jnp.dot(
            jnp.concatenate([high, low], axis=1),
            jnp.concatenate([col_place[...], col_place[...]], axis=0),
            preferred_element_type=jnp.float32,
        )
        acc[it, s, 0] = total[:rows_all]
        acc[it, s, 1] = total[rows_all:]

    def fold_start(it, s):
        src = acc.at[it, s]
        for part, pieces in ((1, rim_pieces), (0, mid_pieces)):
            for at, first, length in pieces:
                rows = pl.ds(first, length)
                re, im = (src[c, rows, 0:LANES] for c in range(2))
                col_out[it, FOLD, s, BACK, pl.ds(at, length), :] = pack_high(re, im)
                re, im = (src[c, rows, lane0 + tile : wide] for c in range(2))
                col_out[it, FOLD, s, AHEAD, pl.ds(at, length), :] = pack_low(re, im)
            for direction in (BACK, AHEAD):
                start(col_copy(it, FOLD, s, part, direction))

    def add_cols(it, s, pieces):
        for at, first, length in pieces:
            rows = pl.ds(first, length)
            low = low_lanes((length, LANES))
            got = col_in[it, FOLD, s, AHEAD, pl.ds(at, length), :]
            lanes = slice(lane0, lane0 + LANES)
            acc[it, s, 0, rows, lanes] += jnp.where(low, got, 0.0)
            acc[it, s, 1, rows, lanes] += jnp.where(low, turned(got), 0.0)
            got = col_in[it, FOLD, s, BACK, pl.ds(at, length), :]
            lanes = slice(lane0 + tile - LANES, lane0 + tile)
            acc[it, s, 0, rows, lanes] += jnp.where(low, 0.0, turned(got))
            acc[it, s, 1, rows, lanes] += jnp.where(low, 0.0, got)

    def fold_corners(it, s):
        for direction in (BACK, AHEAD):
            col_copy(it, FOLD, s, 1, direction).wait_recv()
        add_cols(it, s, rim_pieces)
        for direction in (BACK, AHEAD):
            start(fold_rows(it, s, direction))

    def fold_finish(it, s):
        for direction in (BACK, AHEAD):
            col_copy(it, FOLD, s, 0, direction).wait_recv()
        add_cols(it, s, mid_pieces)
        for direction in (BACK, AHEAD):
            fold_rows(it, s, direction).wait_recv()
        last = it == ITERS - 1
        for c in range(2):
            for first in range(0, tile, rim):
                total = acc[it, s, c, pl.ds(rim + first, rim), inner]
                if first == 0:
                    total += row_in[it, s, AHEAD, c]
                if first == tile - rim:
                    total += row_in[it, s, BACK, c]
                new = ext[it, s, c, pl.ds(rim + first, rim), inner] - step_size * total
                if last:
                    grad_ref[s, c, pl.ds(first, rim), :] = total
                    est_ref[s, c, pl.ds(first, rim), :] = new
                else:
                    ext[it + 1, s, c, pl.ds(rim + first, rim), inner] = new

    for s in range(2):
        for direction in (BACK, AHEAD):
            start(halo_rows(0, s, direction))
    for s in range(2):
        for c in range(2):
            ext[0, s, c, rim : rim + tile, inner] = obj_ref[s, c]
        halo_cols(0, s, 0)
    build_picks()

    forward = (right_ref.at[0], left_ref.at[0])
    inverse = (right_ref.at[1], left_ref.at[1])

    for it in range(ITERS):
        halo_corners(it, 0)
        halo_finish(it, 0)
        probe = (probe_ref[0], probe_ref[1])
        prop = (prop_ref[0], prop_ref[1])
        waves = [times(probe, a) for a in crop(it, 0)]
        waves = [times(prop, f) for f in transform(waves, *forward)]
        halo_corners(it, 1)
        phi = transform(waves, *inverse)
        halo_finish(it, 1)
        second = crop(it, 1)
        far = transform([times(p, a) for p, a in zip(phi, second)], *forward)
        resid = []
        for j, (re, im) in enumerate(far):
            excess = re * re + im * im - inten_ref[0, 0, j]
            resid.append((excess * re, excess * im))
        back = transform(resid, *inverse)
        scatter(it, 1, [conj_times(p, b) for p, b in zip(phi, back)])
        fold_start(it, 1)
        waves = transform([conj_times(a, b) for a, b in zip(second, back)], *forward)
        fold_corners(it, 1)
        waves = transform([conj_times(prop, f) for f in waves], *inverse)
        scatter(it, 0, [conj_times(probe, g) for g in waves])
        fold_start(it, 0)
        fold_corners(it, 0)
        fold_finish(it, 1)
        if it + 1 < ITERS:
            halo_start(it + 1, 1)
        fold_finish(it, 0)
        if it + 1 < ITERS:
            halo_start(it + 1, 0)
    for copy in sent:
        copy.wait_send()


def local(sizes, window_starts, slot_counts, intensities, probe_field, kernel_phase, object_field):
    tile = object_field.shape[-1]
    window = sizes[2]
    rim = window // 2
    rows_all = tile + 2 * rim
    wide = tile + 2 * LANES
    slots = intensities.shape[2]
    right, left = fourier_tables(window)
    prop = jnp.stack([jnp.cos(kernel_phase), jnp.sin(kernel_phase)])
    vmem = pl.BlockSpec(memory_space=pltpu.VMEM)
    smem = pl.BlockSpec(memory_space=pltpu.SMEM)
    copies = ITERS * 2 * 2 * 3 * 2
    shape = jax.ShapeDtypeStruct(object_field.shape, jnp.float32)
    return pl.pallas_call(
        functools.partial(kernel, sizes),
        out_shape=(shape, shape),
        in_specs=[smem, smem] + [vmem] * 6,
        out_specs=(vmem, vmem),
        scratch_shapes=[
            pltpu.VMEM((ITERS, 2, 2, rows_all, wide), jnp.float32),
            pltpu.VMEM((ITERS, 2, 2, rows_all, wide), jnp.float32),
            pltpu.VMEM((slots * window, rows_all), jnp.bfloat16),
            pltpu.VMEM((rows_all, slots * window), jnp.bfloat16),
            pltpu.VMEM((wide, slots * window), jnp.bfloat16),
            pltpu.VMEM((slots * window, wide), jnp.bfloat16),
            pltpu.VMEM((ITERS, 2, 2, 2, rows_all, LANES), jnp.float32),
            pltpu.VMEM((ITERS, 2, 2, 2, rows_all, LANES), jnp.float32),
            pltpu.VMEM((ITERS, 2, 2, 2, rim, tile), jnp.float32),
            pltpu.SemaphoreType.DMA((copies,)),
            pltpu.SemaphoreType.DMA((copies,)),
        ],
        compiler_params=pltpu.CompilerParams(
            collective_id=0, has_side_effects=True, vmem_limit_bytes=56 * 1024 * 1024
        ),
    )(
        window_starts,
        slot_counts,
        intensities,
        probe_field,
        prop,
        jnp.asarray(right),
        jnp.asarray(left),
        object_field,
    )


def solution(mesh):
    in_specs = (
        P("gy", "gx", None, None),
        P("gy", "gx"),
        P("gy", "gx", None, None, None),
        P(),
        P(),
        P(None, None, "gy", "gx"),
    )
    out_specs = (P(None, None, "gy", "gx"), P(None, None, "gy", "gx"))

    def run(*args):
        sizes = (mesh.shape["gy"], mesh.shape["gx"], args[3].shape[-1])
        return jax.shard_map(
            functools.partial(local, sizes),
            mesh=mesh,
            in_specs=in_specs,
            out_specs=out_specs,
            check_vma=False,
        )(*args)

    return run
```

profile of v0, /device:TPU:0, one launch (start us, length us, event | category | flops | bytes accessed | tf_op | source)
XLA Modules:
  0.0 96.2 jit_solution(9305662364881598271)
XLA Ops:
  1.3 1.1 %cosine_bitcast_fusion = (f32[1,128,128]{2,1,0:T(8,128)S(1)}, f32[1,128,128]{2,1,0:T(8,128)S(1)}) fusion(f32[128,128]{1,0:T(8,128)} %param.12), kind=kLoop, calls=%fused_computation.2 | loop fusion | bytes 196608 | tf_op jit(solution)/shard_map/stack | solution.py:393
  2.4 0.7 pad_maximum_fusion.prop_ref
  3.0 89.8 %shard_map.95 = (f32[2,2,256,256]{3,2,1,0:T(8,128)}, f32[2,2,256,256]{3,2,1,0:T(8,128)}) custom-call(s32[1,1,2,4]{3,2,1,0:T(2,128)} %starts_ref.1, s32[1,1]{1,0:T(1,128)S(6)} %copy.12.count_ref, f32[1,1,4,128,128]{4,3,2,1,0:T(8,128)} %inten_ref.1, f32[2,128,128]{2,1,0:T(8,128)} %probe_ref.1, f32[2,128,128]{2,1,0:T(8,128)} %pad_maximum_fusion.prop_ref, ...), custom_call_target="tpu_custom_call" | custom-call | tf_op jit(solution)/shard_map/pallas_call | solution.py:398
  92.8 0.0 copy-start
  92.8 2.4 %copy.13 = f32[2,2,256,256]{3,2,1,0:T(8,128)} copy(f32[2,2,256,256]{3,2,1,0:T(8,128)} %get-tuple-element.6) | data formatting | bytes 2097152
  95.2 0.0 copy-done
  95.2 1.0 %copy.14 = f32[2,2,256,256]{3,2,1,0:T(8,128)} copy(f32[2,2,256,256]{3,2,1,0:T(8,128)S(1)} %copy-done) | data formatting | bytes 2097152
Async XLA Ops:
  92.8 2.4 %copy-start = (f32[2,2,256,256]{3,2,1,0:T(8,128)S(1)}, f32[2,2,256,256]{3,2,1,0:T(8,128)}, u32[]{:S(2)}) copy-start(f32[2,2,256,256]{3,2,1,0:T(8,128)} %get-tuple-element.7) | copy-start | bytes 3145732
where the time goes:
time: 96.4 us; the launch traced here: 96.2 us
  Pallas kernels  89.8 us (93%)
  local copies, waits for them, and re-layouts  4.43 us (5%)
  between operations  1.3 us (1%)
    pallas_call x1, Pallas kernels, local(): pl.pallas_call(functools.partial(kernel, sizes), out_shape=(shape, shape)...  89.8 us
    unnamed x4, local copies, waits for them, and re-layouts  3.35 us

commit v1 on v0

--- a/solution.py
+++ b/solution.py
@@ -16,6 +16,7 @@
 step_size = 0.5
 HALO, FOLD = 0, 1
 BACK, AHEAD = 0, 1
+MID, TOP, BOTTOM, ROWS = 0, 1, 2, 3
 
 
 def split(table):
@@ -84,18 +85,29 @@
     return (a[0] * b[0] + a[1] * b[1], a[0] * b[1] - a[1] * b[0])
 
 
+def phasor(angle):
+    x = 0.5 * angle
+    y = x * x
+    sine, cosine = 0.0, 0.0
+    for k in range(7, -1, -1):
+        sine = sine * y + (-1.0) ** k / math.factorial(2 * k + 1)
+        cosine = cosine * y + (-1.0) ** k / math.factorial(2 * k)
+    sine = sine * x
+    return (1.0 - 2.0 * sine * sine, 2.0 * sine * cosine)
+
+
 def kernel(
     sizes,
     starts_ref,
     count_ref,
     inten_ref,
     probe_ref,
-    prop_ref,
+    phase_ref,
     right_ref,
     left_ref,
     obj_ref,
-    est_ref,
-    grad_ref,
+    old_ref,
+    change_ref,
     ext,
     acc,
     row_pick,
@@ -128,8 +140,8 @@
     pl.semaphore_wait(barrier, 4)
 
     def remote(src, dst, it, what, s, part, direction):
-        k = ((((it * 2) + what) * 2 + s) * 3 + part) * 2 + direction
-        dev = ((west, east), (west, east), (up, down))[part][direction]
+        k = ((((it * 2) + what) * 2 + s) * 4 + part) * 2 + direction
+        dev = (up, down)[direction] if part == ROWS else (west, east)[direction]
         return pltpu.make_async_remote_copy(
             src_ref=src,
             dst_ref=dst,
@@ -139,9 +151,15 @@
             device_id_type=MESH,
         )
 
+    pieces = {
+        MID: (0, rim, tile),
+        TOP: (tile, 0, rim),
+        BOTTOM: (tile + rim, tile + rim, rim),
+    }
+    own, rims = (MID,), (TOP, BOTTOM)
+
     def col_copy(it, what, s, part, direction):
-        span = pl.ds(0, tile) if part == 0 else pl.ds(tile, 2 * rim)
-        at = (it, what, s, direction, span)
+        at = (it, what, s, direction, pl.ds(pieces[part][0], pieces[part][2]))
         return remote(col_out.at[at], col_in.at[at], it, what, s, part, direction)
 
     def halo_rows(it, s, direction):
@@ -152,12 +170,12 @@
             src = ext.at[it, s, :, pl.ds(rim + first, rim), pl.ds(lane0, tile)]
         land = tile + rim if direction == BACK else 0
         dst = ext.at[it, s, :, pl.ds(land, rim), pl.ds(lane0, tile)]
-        return remote(src, dst, it, HALO, s, 2, direction)
+        return remote(src, dst, it, HALO, s, ROWS, direction)
 
     def fold_rows(it, s, direction):
         first = 0 if direction == BACK else tile + rim
         src = acc.at[it, s, :, pl.ds(first, rim), pl.ds(lane0, tile)]
-        return remote(src, row_in.at[it, s, direction], it, FOLD, s, 2, direction)
+        return remote(src, row_in.at[it, s, direction], it, FOLD, s, ROWS, direction)
 
     def low_lanes(shape):
         return lax.broadcasted_iota(jnp.int32, shape, 1) < rim
@@ -177,22 +195,22 @@
         copy.start()
         sent.append(copy)
 
-    mid_pieces = ((0, rim, tile),)
-    rim_pieces = ((tile, 0, rim), (tile + rim, tile + rim, rim))
-
     def halo_cols(it, s, part):
-        for at, first, length in mid_pieces if part == 0 else rim_pieces:
-            src = ext.at[it, s]
-            rows = pl.ds(first, length)
-            re, im = (src[c, rows, lane0 : lane0 + LANES] for c in range(2))
-            col_out[it, HALO, s, BACK, pl.ds(at, length), :] = pack_low(re, im)
-            re, im = (src[c, rows, lane0 + tile - LANES : lane0 + tile] for c in range(2))
-            col_out[it, HALO, s, AHEAD, pl.ds(at, length), :] = pack_high(re, im)
+        at, first, length = pieces[part]
+        src = ext.at[it, s]
+        rows = pl.ds(first, length)
+        re, im = (src[c, rows, lane0 : lane0 + LANES] for c in range(2))
+        col_out[it, HALO, s, BACK, pl.ds(at, length), :] = pack_low(re, im)
+        re, im = (src[c, rows, lane0 + tile - LANES : lane0 + tile] for c in range(2))
+        col_out[it, HALO, s, AHEAD, pl.ds(at, length), :] = pack_high(re, im)
         for direction in (BACK, AHEAD):
             start(col_copy(it, HALO, s, part, direction))
 
-    def unpack_halo(it, s):
-        for at, first, length in mid_pieces + rim_pieces:
+    def halo_arrive(it, s, parts):
+        for part in parts:
+            at, first, length = pieces[part]
+            for direction in (BACK, AHEAD):
+                col_copy(it, HALO, s, part, direction).wait_recv()
             rows = pl.ds(first, length)
             got = col_in[it, HALO, s, AHEAD, pl.ds(at, length), :]
             ext[it, s, 0, rows, 0:LANES] = turned(got)
@@ -204,40 +222,47 @@
     def halo_start(it, s):
         for direction in (BACK, AHEAD):
             start(halo_rows(it, s, direction))
-        halo_cols(it, s, 0)
+        halo_cols(it, s, MID)
 
     def halo_corners(it, s):
-        for direction in (BACK, AHEAD):
+        for direction, part in ((BACK, BOTTOM), (AHEAD, TOP)):
             halo_rows(it, s, direction).wait_recv()
-        halo_cols(it, s, 1)
-
-    def halo_finish(it, s):
-        for part in (0, 1):
-            for direction in (BACK, AHEAD):
-                col_copy(it, HALO, s, part, direction).wait_recv()
-        unpack_halo(it, s)
+            halo_cols(it, s, part)
 
     def ones(mask):
         return jnp.where(mask, 1.0, 0.0).astype(jnp.bfloat16)
+
+    def ext_row(k):
+        return jnp.where(k < tile, k + rim, jnp.where(k < tile + rim, k - tile, k))
 
     def build_picks():
         for j in range(slots):
             row = starts_ref[0, 0, 0, j] + rim
             col = starts_ref[0, 0, 1, j] + lane0
             span = slice(j * window, (j + 1) * window)
-            for ref, at, first, shape, sign in (
-                (row_pick, (span, slice(None)), row, (window, rows_all), 1),
-                (row_place, (slice(None), span), row, (rows_all, window), -1),
-                (col_pick, (slice(None), span), col, (wide, window), -1),
-                (col_place, (span, slice(None)), col, (window, wide), 1),
-            ):
-                across = lax.broadcasted_iota(jnp.int32, shape, 1)
-                along = lax.broadcasted_iota(jnp.int32, shape, 0)
+
+            def build(shape, large, small, first, order):
+                large = order(lax.broadcasted_iota(jnp.int32, shape, large))
+                small = lax.broadcasted_iota(jnp.int32, shape, small)
                 live = jnp.full(shape, count_ref[0, 0], jnp.int32) > j
-                ref[at] = ones((sign * (across - along) == first) & live)
-
-    def crop(it, s):
-        both = jnp.concatenate([ext[it, s, c] for c in range(2)], axis=0)
+                return ones((large - small == first) & live)
+
+            row_pick[span, :] = build((window, rows_all), 1, 0, row, ext_row)
+            row_place[:, span] = build((rows_all, window), 0, 1, row, ext_row)
+            col_pick[:, span] = build((wide, window), 0, 1, col, lambda k: k)
+            col_place[span, :] = build((window, wide), 1, 0, col, lambda k: k)
+
+    def crop(it, s, parts):
+        begin = pieces[parts[0]][0]
+        height = sum(pieces[part][2] for part in parts)
+        both = jnp.concatenate(
+            [
+                ext[it, s, c, pl.ds(pieces[part][1], pieces[part][2]), :]
+                for c in range(2)
+                for part in parts
+            ],
+            axis=0,
+        )
         high, low = halves(both)
         cols = jnp.dot(
             jnp.concatenate([high, low], axis=1),
@@ -248,9 +273,9 @@
         out = []
         for j in range(slots):
             span = slice(j * window, (j + 1) * window)
-            pick = row_pick[span, :]
+            pick = row_pick[span, begin : begin + height]
             field = [
-                jnp.concatenate([part[:rows_all, span], part[rows_all:, span]], axis=1)
+                jnp.concatenate([part[:height, span], part[height:, span]], axis=1)
                 for part in (high, low)
             ]
             got = jnp.dot(
@@ -261,41 +286,47 @@
             out.append((got[:, :window], got[:, window:]))
         return out
 
-    def scatter(it, s, grads):
-        parts = []
+    def both_crops(inside, outside):
+        return [(a[0] + b[0], a[1] + b[1]) for a, b in zip(inside, outside)]
+
+    def scatter(it, s, grads, parts):
+        begin = pieces[parts[0]][0]
+        height = sum(pieces[part][2] for part in parts)
+        placed = []
         for j in range(slots):
-            span = slice(j * window, (j + 1) * window)
-            put = row_place[:, span]
+            put = row_place[begin : begin + height, j * window : (j + 1) * window]
             high, low = halves(jnp.concatenate(grads[j], axis=1))
             got = jnp.dot(
                 jnp.concatenate([put, put], axis=1),
                 jnp.concatenate([high, low], axis=0),
                 preferred_element_type=jnp.float32,
             )
-            parts.append(jnp.concatenate([got[:, :window], got[:, window:]], axis=0))
-        high, low = halves(jnp.concatenate(parts, axis=1))
+            placed.append(jnp.concatenate([got[:, :window], got[:, window:]], axis=0))
+        high, low = halves(jnp.concatenate(placed, axis=1))
         total = jnp.dot(
             jnp.concatenate([high, low], axis=1),
             jnp.concatenate([col_place[...], col_place[...]], axis=0),
             preferred_element_type=jnp.float32,
         )
-        acc[it, s, 0] = total[:rows_all]
-        acc[it, s, 1] = total[rows_all:]
-
-    def fold_start(it, s):
+        for c in range(2):
+            for part in parts:
+                at, first, length = pieces[part]
+                at += c * height - begin
+                acc[it, s, c, pl.ds(first, length), :] = total[at : at + length]
         src = acc.at[it, s]
-        for part, pieces in ((1, rim_pieces), (0, mid_pieces)):
-            for at, first, length in pieces:
-                rows = pl.ds(first, length)
-                re, im = (src[c, rows, 0:LANES] for c in range(2))
-                col_out[it, FOLD, s, BACK, pl.ds(at, length), :] = pack_high(re, im)
-                re, im = (src[c, rows, lane0 + tile : wide] for c in range(2))
-                col_out[it, FOLD, s, AHEAD, pl.ds(at, length), :] = pack_low(re, im)
+        for part in parts:
+            at, first, length = pieces[part]
+            rows = pl.ds(first, length)
+            re, im = (src[c, rows, 0:LANES] for c in range(2))
+            col_out[it, FOLD, s, BACK, pl.ds(at, length), :] = pack_high(re, im)
+            re, im = (src[c, rows, lane0 + tile : wide] for c in range(2))
+            col_out[it, FOLD, s, AHEAD, pl.ds(at, length), :] = pack_low(re, im)
             for direction in (BACK, AHEAD):
                 start(col_copy(it, FOLD, s, part, direction))
 
-    def add_cols(it, s, pieces):
-        for at, first, length in pieces:
+    def add_cols(it, s, parts):
+        for part in parts:
+            at, first, length = pieces[part]
             rows = pl.ds(first, length)
             low = low_lanes((length, LANES))
             got = col_in[it, FOLD, s, AHEAD, pl.ds(at, length), :]
@@ -308,16 +339,16 @@
             acc[it, s, 1, rows, lanes] += jnp.where(low, 0.0, got)
 
     def fold_corners(it, s):
-        for direction in (BACK, AHEAD):
-            col_copy(it, FOLD, s, 1, direction).wait_recv()
-        add_cols(it, s, rim_pieces)
-        for direction in (BACK, AHEAD):
+        for direction, part in ((BACK, TOP), (AHEAD, BOTTOM)):
+            for side in (BACK, AHEAD):
+                col_copy(it, FOLD, s, part, side).wait_recv()
+            add_cols(it, s, (part,))
             start(fold_rows(it, s, direction))
 
     def fold_finish(it, s):
         for direction in (BACK, AHEAD):
-            col_copy(it, FOLD, s, 0, direction).wait_recv()
-        add_cols(it, s, mid_pieces)
+            col_copy(it, FOLD, s, MID, direction).wait_recv()
+        add_cols(it, s, own)
         for direction in (BACK, AHEAD):
             fold_rows(it, s, direction).wait_recv()
         last = it == ITERS - 1
@@ -328,12 +359,13 @@
                     total += row_in[it, s, AHEAD, c]
                 if first == tile - rim:
                     total += row_in[it, s, BACK, c]
-                new = ext[it, s, c, pl.ds(rim + first, rim), inner] - step_size * total
+                change = step_size * total
+                old = ext[it, s, c, pl.ds(rim + first, rim), inner]
                 if last:
-                    grad_ref[s, c, pl.ds(first, rim), :] = total
-                    est_ref[s, c, pl.ds(first, rim), :] = new
+                    change_ref[s, c, pl.ds(first, rim), :] = change
+                    old_ref[s, c, pl.ds(first, rim), :] = old
                 else:
-                    ext[it + 1, s, c, pl.ds(rim + first, rim), inner] = new
+                    ext[it + 1, s, c, pl.ds(rim + first, rim), inner] = old - change
 
     for s in range(2):
         for direction in (BACK, AHEAD):
@@ -341,36 +373,44 @@
     for s in range(2):
         for c in range(2):
             ext[0, s, c, rim : rim + tile, inner] = obj_ref[s, c]
-        halo_cols(0, s, 0)
+        halo_cols(0, s, MID)
     build_picks()
 
     forward = (right_ref.at[0], left_ref.at[0])
     inverse = (right_ref.at[1], left_ref.at[1])
 
+    prop = phasor(phase_ref[...])
+    probe = (probe_ref[0], probe_ref[1])
+
     for it in range(ITERS):
+        halo_arrive(it, 0, own)
         halo_corners(it, 0)
-        halo_finish(it, 0)
-        probe = (probe_ref[0], probe_ref[1])
-        prop = (prop_ref[0], prop_ref[1])
-        waves = [times(probe, a) for a in crop(it, 0)]
+        inside = crop(it, 0, own)
+        halo_arrive(it, 0, rims)
+        first = both_crops(inside, crop(it, 0, rims))
+        waves = [times(probe, a) for a in first]
         waves = [times(prop, f) for f in transform(waves, *forward)]
         halo_corners(it, 1)
         phi = transform(waves, *inverse)
-        halo_finish(it, 1)
-        second = crop(it, 1)
+        halo_arrive(it, 1, own)
+        inside = crop(it, 1, own)
+        halo_arrive(it, 1, rims)
+        second = both_crops(inside, crop(it, 1, rims))
         far = transform([times(p, a) for p, a in zip(phi, second)], *forward)
         resid = []
         for j, (re, im) in enumerate(far):
             excess = re * re + im * im - inten_ref[0, 0, j]
             resid.append((excess * re, excess * im))
         back = transform(resid, *inverse)
-        scatter(it, 1, [conj_times(p, b) for p, b in zip(phi, back)])
-        fold_start(it, 1)
+        grads = [conj_times(p, b) for p, b in zip(phi, back)]
+        scatter(it, 1, grads, rims)
+        scatter(it, 1, grads, own)
         waves = transform([conj_times(a, b) for a, b in zip(second, back)], *forward)
         fold_corners(it, 1)
         waves = transform([conj_times(prop, f) for f in waves], *inverse)
-        scatter(it, 0, [conj_times(probe, g) for g in waves])
-        fold_start(it, 0)
+        grads = [conj_times(probe, g) for g in waves]
+        scatter(it, 0, grads, rims)
+        scatter(it, 0, grads, own)
         fold_corners(it, 0)
         fold_finish(it, 1)
         if it + 1 < ITERS:
@@ -390,12 +430,11 @@
     wide = tile + 2 * LANES
     slots = intensities.shape[2]
     right, left = fourier_tables(window)
-    prop = jnp.stack([jnp.cos(kernel_phase), jnp.sin(kernel_phase)])
     vmem = pl.BlockSpec(memory_space=pltpu.VMEM)
     smem = pl.BlockSpec(memory_space=pltpu.SMEM)
-    copies = ITERS * 2 * 2 * 3 * 2
+    copies = ITERS * 2 * 2 * 4 * 2
     shape = jax.ShapeDtypeStruct(object_field.shape, jnp.float32)
-    return pl.pallas_call(
+    old, change = pl.pallas_call(
         functools.partial(kernel, sizes),
         out_shape=(shape, shape),
         in_specs=[smem, smem] + [vmem] * 6,
@@ -421,11 +460,12 @@
         slot_counts,
         intensities,
         probe_field,
-        prop,
+        kernel_phase,
         jnp.asarray(right),
         jnp.asarray(left),
         object_field,
     )
+    return old - change, change / step_size
 
 
 def solution(mesh):

time: 96.4 us -> 88.2 us (0.915)
  Pallas kernels: 89.8 us -> 83.7 us
  local copies, waits for them, and re-layouts: 4.43 us -> 0 us
  other arithmetic: 0.67 us -> 3.06 us
    pallas_call x1, Pallas kernels: 89.8 us -> 83.7 us  [local(): pl.pallas_call(functools.partial(kernel, sizes), out_shape=(shape, shape)...]
    unnamed x4 -> x0, local copies, waits for them, and re-layouts: 3.35 us -> none
    div x0 -> x1, other arithmetic: none -> 3.06 us  [local(): return (old - change, change / step_size)]
    another operation x1 -> x0, local copies, waits for them, and re-layouts: 1.08 us -> none  [local(): prop = jnp.stack([jnp.cos(kernel_phase), jnp.sin(kernel_phase)])]
where the time goes in v1:
time: 88.2 us; the launch traced here: 88 us
  Pallas kernels  83.7 us (95%)
  other arithmetic  3.06 us (3%)
  between operations  1.28 us (1%)
    pallas_call x1, Pallas kernels, local(): pl.pallas_call(functools.partial(kernel, sizes), out_shape=(shape, shape)...  83.7 us
    div x1, other arithmetic, local(): return (old - change, change / step_size)  3.06 us

profile of v1, /device:TPU:0, one launch (start us, length us, event | category | flops | bytes accessed | tf_op | source)
XLA Modules:
  0.0 88.0 jit_solution(13388104268630979862)
XLA Ops:
  1.3 83.7 %shard_map.95 = (f32[2,2,256,256]{3,2,1,0:T(8,128)}, f32[2,2,256,256]{3,2,1,0:T(8,128)}) custom-call(s32[1,1,2,4]{3,2,1,0:T(2,128)} %starts_ref.1, s32[1,1]{1,0:T(1,128)S(6)} %copy.10.count_ref, f32[1,1,4,128,128]{4,3,2,1,0:T(8,128)} %inten_ref.1, f32[2,128,128]{2,1,0:T(8,128)} %probe_ref.1, f32[128,128]{1,0:T(8,128)} %phase_ref.1, ...), custom_call_target="tpu_custom_call" | custom-call | tf_op jit(solution)/shard_map/pallas_call | solution.py:437
  84.9 3.1 %broadcast_multiply_fusion = (f32[2,2,256,256]{3,2,1,0:T(8,128)}, f32[2,2,256,256]{3,2,1,0:T(8,128)}) fusion(f32[2,2,256,256]{3,2,1,0:T(8,128)} %get-tuple-element.5, f32[2,2,256,256]{3,2,1,0:T(8,128)} %get-tuple-element.4), kind=kLoop, calls=%fused_computation | loop fusion | flops 524288 | bytes 4194304 | tf_op jit(solution)/shard_map/div | solution.py:468

commit v2 on v1

--- a/solution.py
+++ b/solution.py
@@ -413,11 +413,10 @@
         scatter(it, 0, grads, own)
         fold_corners(it, 0)
         fold_finish(it, 1)
-        if it + 1 < ITERS:
-            halo_start(it + 1, 1)
         fold_finish(it, 0)
         if it + 1 < ITERS:
             halo_start(it + 1, 0)
+            halo_start(it + 1, 1)
     for copy in sent:
         copy.wait_send()
 

time: 88.2 us -> 85.1 us (0.965)
  Pallas kernels: 83.7 us -> 80.6 us
    pallas_call x1, Pallas kernels: 83.7 us -> 80.6 us  [local(): pl.pallas_call(functools.partial(kernel, sizes), out_shape=(shape, shape)...]
where the time goes in v2:
time: 85.1 us; the launch traced here: 84.9 us
  Pallas kernels  80.6 us (95%)
  other arithmetic  3.06 us (4%)
  between operations  1.28 us (2%)
    pallas_call x1, Pallas kernels, local(): pl.pallas_call(functools.partial(kernel, sizes), out_shape=(shape, shape)...  80.6 us
    div x1, other arithmetic, local(): return (old - change, change / step_size)  3.06 us

profile of v2, /device:TPU:0, one launch (start us, length us, event | category | flops | bytes accessed | tf_op | source)
XLA Modules:
  0.0 84.9 jit_solution(7511874829077652131)
XLA Ops:
  1.3 80.6 %shard_map.95 = (f32[2,2,256,256]{3,2,1,0:T(8,128)}, f32[2,2,256,256]{3,2,1,0:T(8,128)}) custom-call(s32[1,1,2,4]{3,2,1,0:T(2,128)} %starts_ref.1, s32[1,1]{1,0:T(1,128)S(6)} %copy.10.count_ref, f32[1,1,4,128,128]{4,3,2,1,0:T(8,128)} %inten_ref.1, f32[2,128,128]{2,1,0:T(8,128)} %probe_ref.1, f32[128,128]{1,0:T(8,128)} %phase_ref.1, ...), custom_call_target="tpu_custom_call" | custom-call | tf_op jit(solution)/shard_map/pallas_call | solution.py:436
  81.9 3.1 %broadcast_multiply_fusion = (f32[2,2,256,256]{3,2,1,0:T(8,128)}, f32[2,2,256,256]{3,2,1,0:T(8,128)}) fusion(f32[2,2,256,256]{3,2,1,0:T(8,128)} %get-tuple-element.5, f32[2,2,256,256]{3,2,1,0:T(8,128)} %get-tuple-element.4), kind=kLoop, calls=%fused_computation | loop fusion | flops 524288 | bytes 4194304 | tf_op jit(solution)/shard_map/div | solution.py:467
